TPU v7x, 32 devices: a whole 2x2x4 slice. The times are simulated.
32 devices in a mesh: fsdp: 4 (over z), ctx: 4 (over y, x), tp: 2 (over core).
Axes of the slice: x: 2, y: 2, z: 4, core: 2. Of those that a mesh axis runs over, the one named last changes fastest.
Arguments:
- tokens: bfloat16 [4096, 1024], P(('fsdp', 'ctx')), may hold values from -6 to 6
- lengths: int32 [4, 4], P('fsdp'), may hold values from 1 to 959, as said below
- norm_gain: bfloat16 [1024], P('fsdp'), may hold values from 0.5 to 1.5
- qkv_weight: bfloat16 [3, 1024, 1024], P(None, 'fsdp', 'tp'), may hold values from -0.1875 to 0.1875
- beta_weight: bfloat16 [1024, 8], P('fsdp', 'tp'), may hold values from -0.1875 to 0.1875
- conv_weight: bfloat16 [3, 4, 8, 128], P(None, None, 'tp', 'fsdp'), may hold values from -3 to 3
- head_gain: bfloat16 [128], P('fsdp'), may hold values from 0.5 to 1.5
- out_weight: bfloat16 [1024, 1024], P('tp', 'fsdp'), may hold values from -0.1875 to 0.1875
- mlp_gain: bfloat16 [1024], P('fsdp'), may hold values from 0.5 to 1.5
- gate_up_weight: bfloat16 [2, 1024, 2816], P(None, 'fsdp', 'tp'), may hold values from -0.1875 to 0.1875
- down_weight: bfloat16 [2816, 1024], P('tp', 'fsdp'), may hold values from -0.15625 to 0.15625
- cotangent: bfloat16 [4096, 1024], P(('fsdp', 'ctx')), may hold values from -6 to 6
Outputs:
- layer_out: bfloat16 [4096, 1024], P(('fsdp', 'ctx'))
- input_grad: float32 [4096, 1024], P(('fsdp', 'ctx'))
- norm_gain_grad: float32 [1024], P('fsdp')
- qkv_grad: float32 [3, 1024, 1024], P(None, 'fsdp', 'tp')
- beta_grad: float32 [1024, 8], P('fsdp', 'tp')
- conv_grad: float32 [3, 4, 8, 128], P(None, None, 'tp', 'fsdp')
- head_gain_grad: float32 [128], P('fsdp')
- out_grad: float32 [1024, 1024], P('tp', 'fsdp')
- mlp_gain_grad: float32 [1024], P('fsdp')
- gate_up_grad: float32 [2, 1024, 2816], P(None, 'fsdp', 'tp')
- down_grad: float32 [2816, 1024], P('tp', 'fsdp')
- rms: float32 [5], replicated
Inputs may be any that keep to these rules, and one draw needn't show every extreme that they name: Row g lists the 4 sequence lengths of stream g in order; they sum to at most 1024, the remaining slots at the end are padding. The second sequence of each stream ends at slot 960, so it includes a slot of the first and of the last of its 4 blocks of 256 slots.
All inputs are finite; a program needn't handle non-finite values.
Results may differ from a plain program's by a relative error of at most 0.012.
The roundings to bfloat16 on the way count: a program that leaves them out, or rounds other values in their place, can miss the bound.
Values may be sent and summed in bfloat16 or wider, within the bound.
No kernel may reach another device: no remote copies, remote signals or barrier semaphores. Data moves between devices by JAX's collectives and lax.ppermute only.
A program may use at most 128 MiB of HBM per device.

v0:
```python
import jax
import jax.numpy as jnp
from jax import lax
from jax.sharding import PartitionSpec as P

D = 1024
HD = 128
C = 64
CONV = 4
PRECISE = lax.Precision.HIGHEST
NORM_EPS = 1e-06


def passed_along(value, axis, steps):
    count = lax.axis_size(axis)
    leading, last = (max(0, -steps), min(count, count - steps))
    return lax.ppermute(value, axis, [(source, source + steps) for source in range(leading, last)])


def product(form, left, right):
    return jnp.einsum(form, left, right, precision=PRECISE)


def rounded(values):
    return lax.optimization_barrier(values.astype(jnp.bfloat16)).astype(jnp.float32)


def rms_norm(values, gain):
    return values * lax.rsqrt(jnp.mean(values * values, -1, keepdims=True) + NORM_EPS) * gain


def norm_back(values, gain, grad):
    ratio = lax.rsqrt(jnp.mean(values * values, -1, keepdims=True) + NORM_EPS)
    scaled = values * ratio
    weighted = grad * gain
    value_grad = ratio * (weighted - scaled * jnp.mean(weighted * scaled, -1, keepdims=True))
    gain_grad = jnp.sum((grad * scaled).reshape(-1, values.shape[-1]), 0)
    return (value_grad, gain_grad)


def l2_norm(values):
    return values * lax.rsqrt(jnp.sum(values * values, -1, keepdims=True) + NORM_EPS)


def seq_layout(lengths_row, first, row_count):
    ends = jnp.cumsum(lengths_row)
    places = first + jnp.arange(row_count, dtype=jnp.int32)
    passed = ends[None, :] <= places[:, None]
    begins = jnp.max(jnp.where(passed, ends[None, :], 0), -1)
    seg_ids = jnp.sum(passed.astype(jnp.int32), -1)
    valid = (places < ends[-1]).astype(jnp.float32)
    resets = places == begins
    offsets = places[:, None] - (CONV - 1) + jnp.arange(CONV, dtype=jnp.int32)[None, :]
    taps = (offsets >= begins[:, None]).astype(jnp.float32)
    return (seg_ids, resets, valid, taps)


def block_masks(seg_ids, resets):
    seg_blocks = seg_ids.reshape(-1, C)
    same_seq = (seg_blocks[:, :, None] == seg_blocks[:, None, :]).astype(jnp.float32)
    reset_count = jnp.cumsum(resets.reshape(-1, C).astype(jnp.int32), -1)
    carried = (reset_count == 0).astype(jnp.float32)
    return (same_seq, carried)


def conv_heads(extended, conv_taps, taps):
    row_count = taps.shape[0]
    total = jnp.zeros((row_count,) + extended.shape[1:], jnp.float32)
    for offset in range(CONV):
        total = (
            total
            + extended[offset : offset + row_count]
            * conv_taps[:, offset][None]
            * taps[:, offset][:, None, None]
        )
    activated = jax.nn.silu(total)
    head_count = extended.shape[2] // HD
    split_rows = activated.reshape(row_count, 3, head_count, HD)
    return (l2_norm(split_rows[:, 0]), l2_norm(split_rows[:, 1]), split_rows[:, 2])


def to_blocks(values):
    return values.reshape(values.shape[0] // C, C, values.shape[1], values.shape[2]).transpose(
        2, 0, 1, 3
    )


def beta_blocks(values):
    return values.reshape(values.shape[0] // C, C, values.shape[1]).transpose(2, 0, 1)


def from_blocks(values):
    return values.transpose(1, 2, 0, 3).reshape(-1, values.shape[0], values.shape[3])


def unit_inverse(lower):
    size_now = lower.shape[-1]
    identity = jnp.eye(size_now, dtype=jnp.float32)
    inverse = identity - lower
    power = lower
    span = 2
    while span < size_now:
        power = product("...ij,...jk->...ik", power, power)
        inverse = product("...ij,...jk->...ik", inverse, identity + power)
        span = span * 2
    return inverse


def block_terms(queries, key_rows, value_rows, beta_rows, same_seq, carried):
    wide = key_rows.shape[-1]
    last_seg = same_seq[:, -1, :]
    key_gram = product("hncd,hnmd->hncm", key_rows, key_rows)
    lower = jnp.tril(beta_rows[..., :, None] * key_gram * same_seq, -1)
    inverse = unit_inverse(lower)
    stacked = beta_rows[..., None] * jnp.concatenate([key_rows, value_rows], -1)
    solved = product("hncm,hnmd->hncd", inverse, stacked)
    w_part = solved[..., :wide]
    u_part = solved[..., wide:]
    query_key = jnp.tril(product("hncd,hnmd->hncm", queries, key_rows) * same_seq)
    keep_all = carried[:, -1]
    trans = keep_all[:, None, None] * jnp.eye(wide, dtype=jnp.float32) - product(
        "hnci,hncj->hnij", w_part * (carried * last_seg)[..., None], key_rows
    )
    push = product("hnci,hncj->hnij", u_part * last_seg[..., None], key_rows)
    return (w_part, u_part, query_key, queries, trans, push)


def run_blocks(terms, carried, start_state):
    sequenced = tuple((jnp.moveaxis(piece, 1, 0) for piece in terms)) + (carried,)

    def advance(state, pieces):
        w_now, u_now, qk_now, q_now, trans_now, push_now, carry_now = pieces
        carry_col = carry_now[None, :, None]
        from_state = product("hcd,hvd->hcv", w_now, state)
        fresh = u_now - carry_col * from_state
        output = carry_col * product("hcd,hvd->hcv", q_now, state) + product(
            "hcm,hmv->hcv", qk_now, fresh
        )
        following = product("hvk,hkj->hvj", state, trans_now) + push_now
        return (following, output)

    final_state, outputs = lax.scan(advance, start_state, sequenced)
    return (jnp.moveaxis(outputs, 0, 1), final_state)


def join_maps(earlier, later):
    return (
        product("hik,hkj->hij", earlier[0], later[0]),
        product("hvk,hkj->hvj", earlier[1], later[0]) + later[1],
    )


def row_total(values, valid):
    return jnp.sum(valid * jnp.sum(values * values, -1))


def local(
    tokens,
    lengths,
    norm_gain,
    qkv_weight,
    beta_weight,
    conv_weight,
    head_gain,
    out_weight,
    mlp_gain,
    gate_up_weight,
    down_weight,
    cotangent,
):
    row_count = tokens.shape[0]
    ctx_count = lax.axis_size("ctx")
    fsdp_count = lax.axis_size("fsdp")
    seg_ids, resets, valid, taps = seq_layout(
        lengths[0], lax.axis_index("ctx") * row_count, row_count
    )
    same_seq, carried = block_masks(seg_ids, resets)
    gathered = (
        lax.all_gather(norm_gain, "fsdp", axis=0, tiled=True),
        lax.all_gather(qkv_weight, "fsdp", axis=1, tiled=True),
        lax.all_gather(beta_weight, "fsdp", axis=0, tiled=True),
        lax.all_gather(conv_weight, "fsdp", axis=3, tiled=True),
        lax.all_gather(head_gain, "fsdp", axis=0, tiled=True),
        lax.all_gather(out_weight, "fsdp", axis=1, tiled=True),
        lax.all_gather(mlp_gain, "fsdp", axis=0, tiled=True),
        lax.all_gather(gate_up_weight, "fsdp", axis=1, tiled=True),
        lax.all_gather(down_weight, "fsdp", axis=1, tiled=True),
    )
    (
        first_gain,
        qkv_full,
        beta_full,
        conv_full,
        head_full,
        out_full,
        second_gain,
        gate_up_full,
        down_full,
    ) = gathered
    heads_local = beta_full.shape[1]
    width_local = qkv_full.shape[2]
    x_wide = tokens.astype(jnp.float32)
    first_f = first_gain.astype(jnp.float32)
    second_f = second_gain.astype(jnp.float32)
    head_f = head_full.astype(jnp.float32)
    normed_in = rms_norm(x_wide, first_f).astype(jnp.bfloat16)
    projected = jnp.einsum(
        "td,idk->tik", normed_in, qkv_full, preferred_element_type=jnp.float32
    ).astype(jnp.bfloat16)
    beta_rows = jax.nn.sigmoid(jnp.dot(normed_in, beta_full, preferred_element_type=jnp.float32))
    rim_rows = passed_along(projected[row_count - (CONV - 1) :], "ctx", 1)
    extended = jnp.concatenate([rim_rows, projected], 0).astype(jnp.float32)
    conv_local = conv_full.reshape(3, CONV, width_local).astype(jnp.float32)

    def conv_part(ext_rows, conv_taps):
        return conv_heads(ext_rows, conv_taps, taps)

    (query_raw, key_raw, value_raw), conv_pull = jax.vjp(conv_part, extended, conv_local)
    queries = rounded(query_raw)
    key_rows = rounded(key_raw)
    value_rows = rounded(value_raw)

    def prepare(query_in, key_in, value_in, beta_in):
        return block_terms(
            to_blocks(query_in) * HD ** (-0.5),
            to_blocks(key_in),
            to_blocks(value_in),
            beta_blocks(beta_in),
            same_seq,
            carried,
        )

    terms, prepare_pull = jax.vjp(prepare, queries, key_rows, value_rows, beta_rows)
    identity = jnp.broadcast_to(jnp.eye(HD, dtype=jnp.float32), (heads_local, HD, HD))
    empty_state = jnp.zeros((heads_local, HD, HD), jnp.float32)

    def compose(accum, pieces):
        return (join_maps(accum, pieces), None)

    (device_map, device_shift), ignored = lax.scan(
        compose,
        (identity, empty_state),
        (jnp.moveaxis(terms[4], 1, 0), jnp.moveaxis(terms[5], 1, 0)),
    )
    incoming = empty_state
    for repeat in range(ctx_count - 1):
        incoming = passed_along(
            product("hvk,hkj->hvj", incoming, device_map) + device_shift, "ctx", 1
        )

    def run_part(term_in, state_in):
        return run_blocks(term_in, carried, state_in)

    (out_blocks, ignored_state), run_pull = jax.vjp(run_part, terms, incoming)
    mixed_out = from_blocks(out_blocks)
    head_normed = rms_norm(mixed_out, head_f).reshape(row_count, width_local).astype(jnp.bfloat16)
    attn_rows = (
        lax.psum(jnp.dot(head_normed, out_full, preferred_element_type=jnp.float32), "tp")
        * valid[:, None]
    )
    middle = x_wide + attn_rows
    normed_mid = rms_norm(middle, second_f).astype(jnp.bfloat16)
    gate_up = jnp.einsum(
        "td,idf->tif", normed_mid, gate_up_full, preferred_element_type=jnp.float32
    )
    gate_rows = gate_up[:, 0]
    up_rows = gate_up[:, 1]
    activated = (jax.nn.silu(gate_rows) * up_rows).astype(jnp.bfloat16)
    ffn_rows = (
        lax.psum(jnp.dot(activated, down_full, preferred_element_type=jnp.float32), "tp")
        * valid[:, None]
    )
    result = middle + ffn_rows
    stat_sums = jnp.stack(
        [
            row_total(x_wide, valid),
            row_total(attn_rows, valid),
            row_total(middle, valid),
            row_total(ffn_rows, valid),
            row_total(result, valid),
            jnp.sum(valid),
        ]
    )
    out_cot = cotangent.astype(jnp.float32)
    ffn_back = (out_cot * valid[:, None]).astype(jnp.bfloat16)
    down_grad = jnp.einsum("tf,td->fd", activated, ffn_back, preferred_element_type=jnp.float32)
    act_grad = jnp.einsum("td,fd->tf", ffn_back, down_full, preferred_element_type=jnp.float32)
    gate_sig = jax.nn.sigmoid(gate_rows)
    up_grad = act_grad * gate_rows * gate_sig
    gate_grad = act_grad * up_rows * gate_sig * (1.0 + gate_rows * (1.0 - gate_sig))
    gate_up_back = jnp.stack([gate_grad, up_grad], 1).astype(jnp.bfloat16)
    gate_up_grad = jnp.einsum(
        "td,tif->idf", normed_mid, gate_up_back, preferred_element_type=jnp.float32
    )
    mid_part = jnp.einsum(
        "tif,idf->td", gate_up_back, gate_up_full, preferred_element_type=jnp.float32
    )
    mid_grad = lax.psum(mid_part, "tp")
    middle_norm_grad, second_gain_grad = norm_back(middle, second_f, mid_grad)
    middle_grad = out_cot + middle_norm_grad
    attn_back = (middle_grad * valid[:, None]).astype(jnp.bfloat16)
    out_grad = jnp.einsum("tk,td->kd", head_normed, attn_back, preferred_element_type=jnp.float32)
    head_in_grad = jnp.einsum(
        "td,kd->tk", attn_back, out_full, preferred_element_type=jnp.float32
    ).reshape(row_count, heads_local, HD)
    mixed_grad, head_gain_part = norm_back(mixed_out, head_f, head_in_grad)
    mixed_blocks = to_blocks(mixed_grad)

    def state_part(state_in):
        return run_blocks(terms, carried, state_in)[0]

    ignored_out, state_pull = jax.vjp(state_part, incoming)
    local_state = state_pull(mixed_blocks)[0]
    map_turned = jnp.swapaxes(device_map, 1, 2)
    outgoing = empty_state
    for repeat in range(ctx_count - 1):
        outgoing = passed_along(
            local_state + product("hvk,hkj->hvj", outgoing, map_turned), "ctx", -1
        )
    term_grads, ignored_grad = run_pull((mixed_blocks, outgoing))
    query_grad, key_grad, value_grad, beta_row_grad = prepare_pull(term_grads)
    logit_grad = (beta_row_grad * beta_rows * (1.0 - beta_rows)).astype(jnp.bfloat16)
    ext_grad, conv_grad_flat = conv_pull((query_grad, key_grad, value_grad))
    back_rim = passed_along(ext_grad[: CONV - 1], "ctx", -1)
    proj_grad = ext_grad[CONV - 1 :] + jnp.concatenate(
        [jnp.zeros((row_count - (CONV - 1),) + back_rim.shape[1:], jnp.float32), back_rim], 0
    )
    proj_back = proj_grad.astype(jnp.bfloat16)
    qkv_grad = jnp.einsum("td,tik->idk", normed_in, proj_back, preferred_element_type=jnp.float32)
    beta_grad = jnp.einsum("td,th->dh", normed_in, logit_grad, preferred_element_type=jnp.float32)
    in_part = jnp.einsum(
        "tik,idk->td", proj_back, qkv_full, preferred_element_type=jnp.float32
    ) + jnp.einsum("th,dh->td", logit_grad, beta_full, preferred_element_type=jnp.float32)
    in_grad, head_gain_grad = lax.psum((in_part, head_gain_part), "tp")
    x_norm_grad, first_gain_grad = norm_back(x_wide, first_f, in_grad)
    input_grad = middle_grad + x_norm_grad
    stat_rows = jnp.broadcast_to(stat_sums[None, :], (fsdp_count, stat_sums.shape[0]))
    conv_grad = conv_grad_flat.reshape(3, CONV, heads_local, HD)
    shares = (
        lax.psum_scatter(first_gain_grad, "fsdp", scatter_dimension=0, tiled=True),
        lax.psum_scatter(qkv_grad, "fsdp", scatter_dimension=1, tiled=True),
        lax.psum_scatter(beta_grad, "fsdp", scatter_dimension=0, tiled=True),
        lax.psum_scatter(conv_grad, "fsdp", scatter_dimension=3, tiled=True),
        lax.psum_scatter(head_gain_grad, "fsdp", scatter_dimension=0, tiled=True),
        lax.psum_scatter(out_grad, "fsdp", scatter_dimension=1, tiled=True),
        lax.psum_scatter(second_gain_grad, "fsdp", scatter_dimension=0, tiled=True),
        lax.psum_scatter(gate_up_grad, "fsdp", scatter_dimension=1, tiled=True),
        lax.psum_scatter(down_grad, "fsdp", scatter_dimension=1, tiled=True),
        lax.psum_scatter(stat_rows, "fsdp", scatter_dimension=0, tiled=True),
    )
    totals = lax.psum(
        (
            shares[0],
            shares[1],
            shares[2],
            shares[3],
            shares[4],
            shares[5],
            shares[6],
            shares[7],
            shares[8],
            shares[9],
        ),
        "ctx",
    )
    stat_total = totals[9][0]
    rms = jnp.sqrt(stat_total[:5] / (stat_total[5] * D))
    return (
        result.astype(jnp.bfloat16),
        input_grad,
        totals[0],
        totals[1],
        totals[2],
        totals[3],
        totals[4],
        totals[5],
        totals[6],
        totals[7],
        totals[8],
        rms,
    )


def solution(mesh):
    return jax.shard_map(
        local,
        mesh=mesh,
        in_specs=(
            P(("fsdp", "ctx"), None),
            P("fsdp", None),
            P("fsdp"),
            P(None, "fsdp", "tp"),
            P("fsdp", "tp"),
            P(None, None, "tp", "fsdp"),
            P("fsdp"),
            P("tp", "fsdp"),
            P("fsdp"),
            P(None, "fsdp", "tp"),
            P("tp", "fsdp"),
            P(("fsdp", "ctx"), None),
        ),
        out_specs=(
            P(("fsdp", "ctx"), None),
            P(("fsdp", "ctx"), None),
            P("fsdp"),
            P(None, "fsdp", "tp"),
            P("fsdp", "tp"),
            P(None, None, "tp", "fsdp"),
            P("fsdp"),
            P("tp", "fsdp"),
            P("fsdp"),
            P(None, "fsdp", "tp"),
            P("tp", "fsdp"),
            P(),
        ),
        check_vma=False,
    )
```

profile of v0, /device:TPU:0, one launch (start us, length us, event | category | flops | bytes accessed | tf_op | source)
XLA Modules:
  0.0 1154.2 jit_solution(13363397626016956386)
XLA Ops:
  10.7 12.6 %all-gather = bf16[4,1,256]{2,1,0:T(2,128)(2,1)S(1)} all-gather(bf16[1,1,256]{2,1,0:T(2,128)(2,1)S(1)} %reshape.331), channel_id=1, replica_groups=mesh['fsdp'=4,'ctx'=4,'tp'=2] {'fsdp'}, dimensions={0}, use_global_device_ids=true | all-gather | bytes 2560 | tf_op jit(solution)/shard_map/all_gather | solution.py:179
  24.0 17.8 %all_gather.30 = bf16[3,4,4,128]{2,1,0,3:T(4,128)(2,1)S(1)} all-gather(bf16[3,4,4,32]{2,1,0,3:T(4,128)(2,1)S(1)} %copy.589), channel_id=1, replica_groups=mesh['fsdp'=4,'ctx'=4,'tp'=2] {'fsdp'}, dimensions={3}, use_global_device_ids=true | all-gather | bytes 15360 | tf_op jit(solution)/shard_map/all_gather | solution.py:182
  42.4 12.2 %all_gather.28 = bf16[1024,4]{0,1:T(4,128)(2,1)S(1)} all-gather(bf16[256,4]{0,1:T(4,128)(2,1)S(1)} %copy-done.132), channel_id=1, replica_groups=mesh['fsdp'=4,'ctx'=4,'tp'=2] {'fsdp'}, dimensions={0}, use_global_device_ids=true | all-gather | bytes 10240 | tf_op jit(solution)/shard_map/all_gather | solution.py:181
  57.8 11.3 all-reduce.14
  70.2 11.6 %all-gather.7.cloned.1.call-done = bf16[3,1024,512]{2,1,0:T(8,128)(2,1)} async-done(((bf16[3,256,512]{2,1,0:T(8,128)(2,1)}), bf16[3,1024,512]{2,1,0:T(8,128)(2,1)}) %all-gather.7.cloned.1.call-update) | async-done | bytes 3145744 | tf_op jit(solution)/shard_map/all_gather | solution.py:180
  127.2 13.8 %while.85 = (s32[]{:T(128)}, f32[4,128,128]{1,2,0:T(8,128)S(1)}, f32[4,128,128]{1,2,0:T(8,128)}, f32[4,4,128,128]{2,3,1,0:T(8,128)S(1)}, f32[4,4,128,128]{2,3,1,0:T(8,128)}, /*index=5*/s32[]{:T(128)}, s32[]{:T(128)}) while((s32[]{:T(128)}, f32[4,128,128]{1,2,0:T(8,128)S(1)}, f32[4,128,128]{1,2,0:T(8,128)}, ...), condition=%wide.region_7.8_spmd.clone, body=%wide.region_6.7_spmd.clone.sunk | while | flops 201457664 | bytes 2884699 | solution.py:240
  173.9 33.4 %while.82 = (s32[]{:T(128)}, f32[4,128,128]{1,2,0:T(8,128)}, f32[4,4,64,128]{3,2,1,0:T(8,128)}, f32[4,4,128,128]{2,3,1,0:T(8,128)S(1)}, f32[4,1,64,1]{2,3,1,0:T(...) while((s32[]{:T(128)}, f32[4,128,128]{1,2,0:T(8,128)}, ...), condition=%wide.region_10.11_spmd, body=%wide.region_9.10_spmd.sunk | while | flops 226689024 | bytes 3937937 | solution.py:142
  216.9 9.6 all-gather.1
  227.7 9.6 all-reduce.28.cloned.1.call-done
  239.1 107.7 %all-gather.11.cloned.1.call-done = bf16[2,1024,1408]{2,1,0:T(8,128)(2,1)} async-done(((bf16[2,256,1408]{2,1,0:T(8,128)(2,1)}), bf16[2,1024,1408]{2,1,0:T(8,128)(2,1)}) %all-gather.11.cloned.1.call-update) | async-done | bytes 5767184 | tf_op jit(solution)/shard_map/all_gather | solution.py:186
  352.7 53.0 %all-gather.13.cloned.1.call-done = bf16[1408,1024]{1,0:T(8,128)(2,1)} async-done(((bf16[1408,256]{1,0:T(8,128)(2,1)}), bf16[1408,1024]{1,0:T(8,128)(2,1)}) %all-gather.13.cloned.1.call-update) | async-done | bytes 2883600 | tf_op jit(solution)/shard_map/all_gather | solution.py:187
  421.6 12.9 %all-reduce.34.cloned.1.call-done = (f32[256,1024]{1,0:T(8,128)}, f32[256,1024]{1,0:T(8,128)}) async-done(((f32[256,1024]{1,0:T(8,128)}, f32[256,1024]{1,0:T(8,128)}), (f32[256,1024]{1,0:T(8,128)}, f32[256,1024]{1,0:T(8,128)})) %all-reduce.34.cloned.1.call-update) | async-done | bytes 2097168 | tf_op jit(solution)/shard_map/psum | solution.py:270
  448.6 22.0 %while.86 = (s32[]{:T(128)}, f32[4,128,128]{1,2,0:T(8,128)}, f32[4,4,128,128]{3,2,1,0:T(8,128)}, f32[4,1,64,1]{2,3,1,0:T(1,128)S(1)}, f32[4,4,64,128]{3,2,1,0:T(...) while((s32[]{:T(128)}, f32[4,128,128]{1,2,0:T(8,128)}, ...), condition=%wide.region_21.22_spmd.clone, body=%wide.region_20.21_spmd.clone.sunk | while | flops 226787328 | bytes 2756239 | solution.py:142
  475.1 9.1 collective-permute-done.4
  486.8 9.3 collective-permute-done.5
  513.9 51.4 %while.84 = (s32[]{:T(128)}, f32[4,128,128]{1,2,0:T(8,128)S(1)}, f32[4,4,64,128]{3,2,0,1:T(8,128)}, f32[4,4,64,128]{3,2,0,1:T(8,128)}, f32[4,4,64,64]{2,3,1,0:T(...) while((s32[]{:T(128)}, f32[4,128,128]{1,2,0:T(8,128)S(1)}, ...), condition=%wide.region_23.24_spmd, body=%wide.region_22.23_spmd.sunk | while | flops 453312512 | bytes 9840861 | solution.py:142
  633.7 93.4 %reduce-scatter.11.cloned.1.call-done = f32[3,256,512]{1,2,0:T(8,128)} async-done(((f32[3,1024,512]{1,2,0:T(8,128)}), f32[3,256,512]{1,2,0:T(8,128)}) %reduce-scatter.11.cloned.1.call-update) | async-done | bytes 1572880 | tf_op jit(solution)/shard_map/reduce_scatter | solution.py:341
  727.1 197.8 %reduce-scatter.15.cloned.1.call-done = f32[2,256,1408]{1,2,0:T(8,128)} async-done(((f32[2,1024,1408]{1,2,0:T(8,128)}), f32[2,256,1408]{1,2,0:T(8,128)}) %reduce-scatter.15.cloned.1.call-update) | async-done | bytes 2883600 | tf_op jit(solution)/shard_map/reduce_scatter | solution.py:347
  931.4 19.1 %reduce-scatter.19.cloned.1.call-done = f32[256,4]{1,0:T(8,128)} async-done(((f32[1024,4]{1,0:T(8,128)}), f32[256,4]{1,0:T(8,128)}) %reduce-scatter.19.cloned.1.call-update) | async-done | bytes 4112
  951.5 19.1 %reduce-scatter.21.cloned.1.call-done = f32[32,48]{1,0:T(8,128)} async-done(((f32[128,48]{1,0:T(8,128)}), f32[32,48]{1,0:T(8,128)}) %reduce-scatter.21.cloned.1.call-update) | async-done | bytes 6160
  971.6 19.7 %all-reduce.30.cloned.1.call-done = f32[256,1024]{1,0:T(8,128)} async-done(((f32[256,1024]{1,0:T(8,128)}), f32[256,1024]{1,0:T(8,128)}) %all-reduce.30.cloned.1.call-update) | async-done | bytes 1048592 | tf_op jit(solution)/shard_map/psum | solution.py:334
  993.1 19.0 %all-reduce.21 = (f32[1024]{0:T(1024)S(1)}, f32[128]{0:T(128)S(1)}, f32[1024]{0:T(1024)S(1)}, f32[4,6]{1,0:T(4,128)S(1)}) all-reduce(f32[1024]{0:T(1024)S(1)} %get-tuple-element.993, f32[128]{0:T(128)S(1)} %multiply_reduce_fusion.10, f32[1024]{0:T(1024)S(1)} %copy-done.116, ...), channel_id=2, replica_groups=mesh['fsdp'=4,'ctx'=4,'tp'=2] {'fsdp'}, use_global_device_ids=true, to_apply=%region_31.32.clone | all-reduce | flops 2200 | bytes 17600
  1015.3 17.8 %all-reduce.19 = (f32[256]{0:T(256)}, f32[256,4]{0,1:T(4,128)}, f32[3,4,4,32]{3,2,1,0:T(4,128)}, f32[32]{0:T(128)}, f32[256]{0:T(256)}, /*index=5*/f32[1,6]{1,0:T(1,128)S(1)}) all-reduce(f32[256]{0:T(256)S(1)} %dynamic-slice.2, f32[256,4]{0,1:T(4,128)S(1)} %copy.747, ...), channel_id=1, replica_groups=mesh['fsdp'=4,'ctx'=4,'tp'=2] {'ctx'}, use_global_device_ids=true, to_apply=%region_32.33 | all-reduce | flops 3110 | bytes 24880 | tf_op jit(solution)/shard_map/psum | solution.py:351
  1036.2 103.1 %all-reduce.32.cloned.1.call-done = (f32[3,256,512]{1,2,0:T(8,128)}, f32[512,256]{1,0:T(8,128)}, f32[2,256,1408]{1,2,0:T(8,128)}, f32[1408,256]{1,0:T(8,128)}) async-done(((f32[3,256,512]{1,2,0:T(8,128)}, f32[512,256]{1,0:T(8,128)}, f32[2,256,1408]{1,2,0:T(8,128)}, f32[1408,256]{1,0:T(8,128)}), (f32[3,256,512]{1,2,0:T(8,128)}, f32[512,256]{1,0:T(8,128)}, f32[2,256,1408]{1,2,0:T(8,128)}, ...) | async-done | bytes 6422544 | tf_op jit(solution)/shard_map/psum | solution.py:351
  (670 shorter events, 371.5 us)
Async XLA Ops:
  7.3 74.5 %all-gather.7.cloned.1.call-start = ((), (), s32[]{:S(2)}) async-start(), calls=%async_computation.6 | async-start | bytes 3932160 | tf_op jit(solution)/shard_map/all_gather | solution.py:180
  8.0 204.4 %all-gather.9.cloned.1.call-start = ((), (), s32[]{:S(2)}) async-start(), calls=%async_computation.7 | async-start | bytes 1310720 | tf_op jit(solution)/shard_map/all_gather | solution.py:184
  8.7 228.6 %all-reduce.28.cloned.1.call-start = ((), (), s32[]{:S(2)}) async-start(), calls=%async_computation.8 | async-start | bytes 2097152 | tf_op jit(solution)/shard_map/psum | solution.py:258
  84.8 4.8 collective-permute-start
  144.7 8.6 collective-permute-start.1
  154.0 8.3 collective-permute-start.2
  162.9 9.0 collective-permute-start.3
  215.1 131.6 %all-gather.11.cloned.1.call-start = ((), (), s32[]{:S(2)}) async-start(), calls=%async_computation.9 | async-start | bytes 7208960 | tf_op jit(solution)/shard_map/all_gather | solution.py:186
  215.7 190.0 %all-gather.13.cloned.1.call-start = ((), (), s32[]{:S(2)}) async-start(), calls=%async_computation.10 | async-start | bytes 3604480 | tf_op jit(solution)/shard_map/all_gather | solution.py:187
  216.3 218.2 %all-reduce.34.cloned.1.call-start = ((), (), s32[]{:S(2)}) async-start(), calls=%async_computation.19 | async-start | bytes 4194304 | tf_op jit(solution)/shard_map/psum | solution.py:270
  239.0 199.4 %copy-start = (f32[256,1024]{1,0:T(8,128)}, f32[256,1024]{1,0:T(8,128)S(1)}, u32[]{:S(2)}) copy-start(f32[256,1024]{1,0:T(8,128)S(1)} %get-tuple-element.1116) | copy-start | bytes 3145732
  239.1 199.4 %copy-start.96 = (f32[256]{0:T(256)}, f32[256]{0:T(256)S(1)}, u32[]{:S(2)}) copy-start(f32[256]{0:T(256)S(1)} %add_rsqrt_fusion.3) | copy-start | bytes 3076
  414.9 218.8 %reduce-scatter.13.cloned.1.call-start = ((), (), s32[]{:S(2)}) async-start(), calls=%async_computation.13 | async-start | bytes 2621440 | tf_op jit(solution)/shard_map/reduce_scatter | solution.py:345
  447.6 186.1 %reduce-scatter.17.cloned.1.call-start = ((), (), s32[]{:S(2)}) async-start(), calls=%async_computation.15 | async-start | bytes 7208960 | tf_op jit(solution)/shard_map/reduce_scatter | solution.py:348
  473.8 10.4 collective-permute-start.4
  485.5 10.6 collective-permute-start.5
  497.2 10.0 collective-permute-start.6
  502.0 225.1 %reduce-scatter.11.cloned.1.call-start = ((), (), s32[]{:S(2)}) async-start(), calls=%async_computation.12 | async-start | bytes 7864320 | tf_op jit(solution)/shard_map/reduce_scatter | solution.py:341
  604.7 6.5 collective-permute-start.7
  614.9 309.9 %reduce-scatter.15.cloned.1.call-start = ((), (), s32[]{:S(2)}) async-start(), calls=%async_computation.14 | async-start | bytes 14417920 | tf_op jit(solution)/shard_map/reduce_scatter | solution.py:347
  624.3 326.3 %reduce-scatter.19.cloned.1.call-start = ((), (), s32[]{:S(2)}) async-start(), calls=%async_computation.16 | async-start | bytes 655360
  627.6 343.0 %reduce-scatter.21.cloned.1.call-start = ((), (), s32[]{:S(2)}) async-start(), calls=%async_computation.17 | async-start | bytes 81920
  629.1 362.2 %all-reduce.30.cloned.1.call-start = ((), (), s32[]{:S(2)}) async-start(), calls=%async_computation.11 | async-start | bytes 2097152 | tf_op jit(solution)/shard_map/psum | solution.py:334
  633.6 505.7 %all-reduce.32.cloned.1.call-start = ((), (), s32[]{:S(2)}) async-start(), calls=%async_computation.18 | async-start | bytes 12845056 | tf_op jit(solution)/shard_map/psum | solution.py:351
  (144 other events, 1544.9 us)
Sparse Core Ops, SparseCore 0:
  9.7 72.0 all-gather.6
  83.3 29.4 all-gather.8
  215.2 22.0 all-reduce.27
  238.8 107.8 all-gather.10
  348.3 57.4 all-gather.12
  415.0 19.4 all-reduce.33
  447.7 45.0 reduce-scatter.12
  502.1 105.3 reduce-scatter.16
  615.1 111.9 reduce-scatter.10
  729.4 195.4 reduce-scatter.14
  927.8 22.6 reduce-scatter.18
  953.3 17.2 reduce-scatter.20
  973.5 17.7 all-reduce.29
  995.5 143.7 all-reduce.31
where the time goes:
time: 1160 us; the launch traced here: 1150 us
  waiting for transfers between devices  684 us (59%)
  matrix products  210 us (18%)
  blocking collectives  103 us (9%)
  local copies, waits for them, and re-layouts  84.7 us (7%)
  other arithmetic  28.9 us (2%)
  starting transfers between devices  24 us (2%)
  between operations  19.1 us (2%)
    reduce_scatter x1, waiting for transfers between devices, local(): lax.psum_scatter(gate_up_grad, 'fsdp', scatter_dimension=1, tiled=True)  198 us
    dot_general x123, matrix products, product(): return jnp.einsum(form, left, right, precision=PRECISE)  163 us
    all_gather x1, waiting for transfers between devices, local(): lax.all_gather(gate_up_weight, 'fsdp', axis=1, tiled=True)  108 us
    psum x1, waiting for transfers between devices, local(): lax.psum((shares[0], shares[1], shares[2], shares[3], shares[4], shares[5...  103 us
    reduce_scatter x1, waiting for transfers between devices, local(): lax.psum_scatter(qkv_grad, 'fsdp', scatter_dimension=1, tiled=True)  93.4 us
    all_gather x1, waiting for transfers between devices, local(): lax.all_gather(down_weight, 'fsdp', axis=1, tiled=True)  53 us
    unnamed x16, waiting for transfers between devices  40.8 us
    ppermute x8, waiting for transfers between devices, passed_along(): lax.ppermute(value, axis, [(source, source + steps) for source in range(l...  34.1 us
  transfers between devices with their start and end apart: 22, of which 18 were waited for; matrix products, arithmetic and copies ran while one was open for 25% of the time, Pallas kernels for 0%

commit v1 on v0

--- a/solution.py
+++ b/solution.py
@@ -168,6 +168,24 @@
     down_weight,
     cotangent,
 ):
+
+    def group_advance(row_data):
+        local_next = lax.axis_size("fsdp")
+        e_next = lax.axis_index("fsdp")
+        arr_next, raw_out, b_now = (local_next, e_next, row_data.shape[1])
+        pages = [j * arr_next if dd == 1 else j for dd, j in enumerate(row_data.shape)]
+        ready = jnp.zeros(pages, row_data.dtype)
+        local_part = lax.dynamic_update_slice_in_dim(ready, row_data, raw_out * b_now, axis=1)
+        for i in range(1, arr_next):
+            p_next = range(arr_next)
+            g_now = map(lambda dd: (dd, (dd + 1) % arr_next), p_next)
+            y1 = list(g_now)
+            row_data = lax.ppermute(row_data, axis_name="fsdp", perm=y1)
+            local_part = lax.dynamic_update_slice_in_dim(
+                local_part, row_data, (raw_out - i) % arr_next * b_now, axis=1
+            )
+        return local_part
+
     row_count = tokens.shape[0]
     ctx_count = lax.axis_size("ctx")
     fsdp_count = lax.axis_size("fsdp")
@@ -184,7 +202,7 @@
         lax.all_gather(out_weight, "fsdp", axis=1, tiled=True),
         lax.all_gather(mlp_gain, "fsdp", axis=0, tiled=True),
         lax.all_gather(gate_up_weight, "fsdp", axis=1, tiled=True),
-        lax.all_gather(down_weight, "fsdp", axis=1, tiled=True),
+        group_advance(down_weight),
     )
     (
         first_gain,

time: 1160 us -> 1120 us (0.966)
  waiting for transfers between devices: 684 us -> 627 us
    all_gather x1 -> x0, waiting for transfers between devices: 53 us -> none  [local(): lax.all_gather(down_weight, 'fsdp', axis=1, tiled=True)]
    ppermute x0 -> x3, waiting for transfers between devices: none -> 41.2 us  [group_advance(): row_data = lax.ppermute(row_data, axis_name='fsdp', perm=y1)]
    all_gather x1, waiting for transfers between devices: 108 us -> 72.2 us  [local(): lax.all_gather(gate_up_weight, 'fsdp', axis=1, tiled=True)]
    unnamed x16 -> x15, waiting for transfers between devices: 40.8 us -> 40.2 us
    unnamed x311 -> x313, local copies, waits for them, and re-layouts: 29.3 us -> 29.6 us
  transfers between devices with their start and end apart: 22 -> 24, of which waited for: 18 -> 18; matrix products, arithmetic and copies ran while one was open for 25% -> 26% of each run, Pallas kernels for 0% -> 0%
where the time goes in v1:
time: 1120 us
  waiting for transfers between devices  627 us (56%)
  matrix products  210 us (19%)
  blocking collectives  110 us (10%)
  local copies, waits for them, and re-layouts  93 us (8%)
  other arithmetic  29.4 us (3%)
  starting transfers between devices  26 us (2%)
  between operations  19.2 us (2%)
    reduce_scatter x1, waiting for transfers between devices, local(): lax.psum_scatter(gate_up_grad, 'fsdp', scatter_dimension=1, tiled=True)  198 us
    dot_general x123, matrix products, product(): return jnp.einsum(form, left, right, precision=PRECISE)  163 us
    psum x1, waiting for transfers between devices, local(): lax.psum((shares[0], shares[1], shares[2], shares[3], shares[4], shares[5...  103 us
    reduce_scatter x1, waiting for transfers between devices, local(): lax.psum_scatter(qkv_grad, 'fsdp', scatter_dimension=1, tiled=True)  93.8 us
    all_gather x1, waiting for transfers between devices, local(): lax.all_gather(gate_up_weight, 'fsdp', axis=1, tiled=True)  72.2 us
    ppermute x3, waiting for transfers between devices, group_advance(): row_data = lax.ppermute(row_data, axis_name='fsdp', perm=y1)  41.2 us
    unnamed x15, waiting for transfers between devices  40.2 us
    ppermute x8, waiting for transfers between devices, passed_along(): lax.ppermute(value, axis, [(source, source + steps) for source in range(l...  34.1 us
  transfers between devices with their start and end apart: 24, of which 18 were waited for; matrix products, arithmetic and copies ran while one was open for 26% of the time, Pallas kernels for 0%

profile of v1, /device:TPU:0, one launch (start us, length us, event | category | flops | bytes accessed | tf_op | source)
XLA Modules:
  0.0 1115.4 jit_solution(15911187758195093619)
XLA Ops:
  11.7 12.6 %all-gather = bf16[4,1,256]{2,1,0:T(2,128)(2,1)S(1)} all-gather(bf16[1,1,256]{2,1,0:T(2,128)(2,1)S(1)} %reshape.331), channel_id=1, replica_groups=mesh['fsdp'=4,'ctx'=4,'tp'=2] {'fsdp'}, dimensions={0}, use_global_device_ids=true | all-gather | bytes 2560 | tf_op jit(solution)/shard_map/all_gather | solution.py:197
  24.5 17.8 %all_gather.27 = bf16[3,4,4,128]{2,1,0,3:T(4,128)(2,1)S(1)} all-gather(bf16[3,4,4,32]{2,1,0,3:T(4,128)(2,1)S(1)} %copy.589), channel_id=1, replica_groups=mesh['fsdp'=4,'ctx'=4,'tp'=2] {'fsdp'}, dimensions={3}, use_global_device_ids=true | all-gather | bytes 15360 | tf_op jit(solution)/shard_map/all_gather | solution.py:200
  42.9 12.1 %all_gather.25 = bf16[1024,4]{0,1:T(4,128)(2,1)S(1)} all-gather(bf16[256,4]{0,1:T(4,128)(2,1)S(1)} %copy-done.133), channel_id=1, replica_groups=mesh['fsdp'=4,'ctx'=4,'tp'=2] {'fsdp'}, dimensions={0}, use_global_device_ids=true | all-gather | bytes 10240 | tf_op jit(solution)/shard_map/all_gather | solution.py:199
  58.2 10.9 all-reduce.14
  70.1 11.9 %all-gather.6.cloned.1.call-done = bf16[3,1024,512]{2,1,0:T(8,128)(2,1)} async-done(((bf16[3,256,512]{2,1,0:T(8,128)(2,1)}), bf16[3,1024,512]{2,1,0:T(8,128)(2,1)}) %all-gather.6.cloned.1.call-update) | async-done | bytes 3145744 | tf_op jit(solution)/shard_map/all_gather | solution.py:198
  127.4 13.8 %while.85 = (s32[]{:T(128)}, f32[4,128,128]{1,2,0:T(8,128)S(1)}, f32[4,128,128]{1,2,0:T(8,128)}, f32[4,4,128,128]{2,3,1,0:T(8,128)S(1)}, f32[4,4,128,128]{2,3,1,0:T(8,128)}, /*index=5*/s32[]{:T(128)}, s32[]{:T(128)}) while((s32[]{:T(128)}, f32[4,128,128]{1,2,0:T(8,128)S(1)}, f32[4,128,128]{1,2,0:T(8,128)}, ...), condition=%wide.region_7.8_spmd.clone, body=%wide.region_6.7_spmd.clone.sunk | while | flops 201457664 | bytes 2884699 | solution.py:258
  174.2 33.3 %while.82 = (s32[]{:T(128)}, f32[4,128,128]{1,2,0:T(8,128)}, f32[4,4,64,128]{3,2,1,0:T(8,128)}, f32[4,4,128,128]{2,3,1,0:T(8,128)S(1)}, f32[4,1,64,1]{2,3,1,0:T(...) while((s32[]{:T(128)}, f32[4,128,128]{1,2,0:T(8,128)}, ...), condition=%wide.region_10.11_spmd, body=%wide.region_9.10_spmd.sunk | while | flops 226689024 | bytes 3937937 | solution.py:142
  216.5 16.7 %collective-permute-done.4 = bf16[1408,256]{1,0:T(8,128)(2,1)} collective-permute-done((bf16[1408,256]{1,0:T(8,128)(2,1)S(1)}, bf16[1408,256]{1,0:T(8,128)(2,1)}, u32[]{:S(2)}, u32[]{:S(2)}) %collective-permute-start.4) | collective-permute-done | bytes 720928 | tf_op jit(solution)/shard_map/ppermute | solution.py:183
  233.8 17.2 %all-gather.1 = bf16[4,1,256]{2,1,0:T(2,128)(2,1)S(1)} all-gather(bf16[1,1,256]{2,1,0:T(2,128)(2,1)S(1)} %reshape.333), channel_id=1, replica_groups=mesh['fsdp'=4,'ctx'=4,'tp'=2] {'fsdp'}, dimensions={0}, use_global_device_ids=true | all-gather | bytes 2560 | tf_op jit(solution)/shard_map/all_gather | solution.py:203
  261.1 24.5 %collective-permute-done.6 = bf16[1408,256]{1,0:T(8,128)(2,1)S(1)} collective-permute-done((bf16[1408,256]{1,0:T(8,128)(2,1)}, bf16[1408,256]{1,0:T(8,128)(2,1)S(1)}, u32[]{:S(2)}, u32[]{:S(2)}) %collective-permute-start.6) | collective-permute-done | bytes 720928 | tf_op jit(solution)/shard_map/ppermute | solution.py:183
  288.2 72.2 %all-gather.10.cloned.1.call-done = bf16[2,1024,1408]{2,1,0:T(8,128)(2,1)} async-done(((bf16[2,256,1408]{2,1,0:T(8,128)(2,1)}), bf16[2,1024,1408]{2,1,0:T(8,128)(2,1)}) %all-gather.10.cloned.1.call-update) | async-done | bytes 5767184 | tf_op jit(solution)/shard_map/all_gather | solution.py:204
  382.5 13.0 %all-reduce.34.cloned.1.call-done = (f32[256,1024]{1,0:T(8,128)}, f32[256,1024]{1,0:T(8,128)}) async-done(((f32[256,1024]{1,0:T(8,128)}, f32[256,1024]{1,0:T(8,128)}), (f32[256,1024]{1,0:T(8,128)}, f32[256,1024]{1,0:T(8,128)})) %all-reduce.34.cloned.1.call-update) | async-done | bytes 2097168 | tf_op jit(solution)/shard_map/psum | solution.py:288
  409.5 21.9 %while.86 = (s32[]{:T(128)}, f32[4,128,128]{1,2,0:T(8,128)}, f32[4,4,128,128]{3,2,1,0:T(8,128)}, f32[4,1,64,1]{2,3,1,0:T(1,128)S(1)}, f32[4,4,64,128]{3,2,1,0:T(...) while((s32[]{:T(128)}, f32[4,128,128]{1,2,0:T(8,128)}, ...), condition=%wide.region_21.22_spmd.clone, body=%wide.region_20.21_spmd.clone.sunk | while | flops 226787328 | bytes 2756239 | solution.py:142
  435.9 9.1 collective-permute-done.7
  447.7 9.2 collective-permute-done.8
  474.6 51.4 %while.84 = (s32[]{:T(128)}, f32[4,128,128]{1,2,0:T(8,128)S(1)}, f32[4,4,64,128]{3,2,0,1:T(8,128)}, f32[4,4,64,128]{3,2,0,1:T(8,128)}, f32[4,4,64,64]{2,3,1,0:T(...) while((s32[]{:T(128)}, f32[4,128,128]{1,2,0:T(8,128)S(1)}, ...), condition=%wide.region_23.24_spmd, body=%wide.region_22.23_spmd.sunk | while | flops 453312512 | bytes 9840861 | solution.py:142
  594.4 93.8 %reduce-scatter.11.cloned.1.call-done = f32[3,256,512]{1,2,0:T(8,128)} async-done(((f32[3,1024,512]{1,2,0:T(8,128)}), f32[3,256,512]{1,2,0:T(8,128)}) %reduce-scatter.11.cloned.1.call-update) | async-done | bytes 1572880 | tf_op jit(solution)/shard_map/reduce_scatter | solution.py:359
  688.1 197.9 %reduce-scatter.15.cloned.1.call-done = f32[2,256,1408]{1,2,0:T(8,128)} async-done(((f32[2,1024,1408]{1,2,0:T(8,128)}), f32[2,256,1408]{1,2,0:T(8,128)}) %reduce-scatter.15.cloned.1.call-update) | async-done | bytes 2883600 | tf_op jit(solution)/shard_map/reduce_scatter | solution.py:365
  892.6 18.9 %reduce-scatter.19.cloned.1.call-done = f32[256,4]{1,0:T(8,128)} async-done(((f32[1024,4]{1,0:T(8,128)}), f32[256,4]{1,0:T(8,128)}) %reduce-scatter.19.cloned.1.call-update) | async-done | bytes 4112
  912.6 19.2 %reduce-scatter.21.cloned.1.call-done = f32[32,48]{1,0:T(8,128)} async-done(((f32[128,48]{1,0:T(8,128)}), f32[32,48]{1,0:T(8,128)}) %reduce-scatter.21.cloned.1.call-update) | async-done | bytes 6160
  932.8 19.6 %all-reduce.30.cloned.1.call-done = f32[256,1024]{1,0:T(8,128)} async-done(((f32[256,1024]{1,0:T(8,128)}), f32[256,1024]{1,0:T(8,128)}) %all-reduce.30.cloned.1.call-update) | async-done | bytes 1048592 | tf_op jit(solution)/shard_map/psum | solution.py:352
  954.1 19.0 %all-reduce.21 = (f32[1024]{0:T(1024)S(1)}, f32[128]{0:T(128)S(1)}, f32[1024]{0:T(1024)S(1)}, f32[4,6]{1,0:T(4,128)S(1)}) all-reduce(f32[1024]{0:T(1024)S(1)} %get-tuple-element.993, f32[128]{0:T(128)S(1)} %multiply_reduce_fusion.10, f32[1024]{0:T(1024)S(1)} %copy-done.117, ...), channel_id=2, replica_groups=mesh['fsdp'=4,'ctx'=4,'tp'=2] {'fsdp'}, use_global_device_ids=true, to_apply=%region_31.32.clone | all-reduce | flops 2200 | bytes 17600
  976.4 17.8 %all-reduce.19 = (f32[256]{0:T(256)}, f32[256,4]{0,1:T(4,128)}, f32[3,4,4,32]{3,2,1,0:T(4,128)}, f32[32]{0:T(128)}, f32[256]{0:T(256)}, /*index=5*/f32[1,6]{1,0:T(1,128)S(1)}) all-reduce(f32[256]{0:T(256)S(1)} %dynamic-slice.2, f32[256,4]{0,1:T(4,128)S(1)} %copy.747, ...), channel_id=1, replica_groups=mesh['fsdp'=4,'ctx'=4,'tp'=2] {'ctx'}, use_global_device_ids=true, to_apply=%region_32.33 | all-reduce | flops 3110 | bytes 24880 | tf_op jit(solution)/shard_map/psum | solution.py:369
  997.3 103.2 %all-reduce.32.cloned.1.call-done = (f32[3,256,512]{1,2,0:T(8,128)}, f32[512,256]{1,0:T(8,128)}, f32[2,256,1408]{1,2,0:T(8,128)}, f32[1408,256]{1,0:T(8,128)}) async-done(((f32[3,256,512]{1,2,0:T(8,128)}, f32[512,256]{1,0:T(8,128)}, f32[2,256,1408]{1,2,0:T(8,128)}, f32[1408,256]{1,0:T(8,128)}), (f32[3,256,512]{1,2,0:T(8,128)}, f32[512,256]{1,0:T(8,128)}, f32[2,256,1408]{1,2,0:T(8,128)}, ...) | async-done | bytes 6422544 | tf_op jit(solution)/shard_map/psum | solution.py:369
  (681 shorter events, 381.5 us)
Async XLA Ops:
  7.2 74.7 %all-gather.6.cloned.1.call-start = ((), (), s32[]{:S(2)}) async-start(), calls=%async_computation.6 | async-start | bytes 3932160 | tf_op jit(solution)/shard_map/all_gather | solution.py:198
  8.0 204.7 %all-gather.8.cloned.1.call-start = ((), (), s32[]{:S(2)}) async-start(), calls=%async_computation.7 | async-start | bytes 1310720 | tf_op jit(solution)/shard_map/all_gather | solution.py:202
  8.7 277.7 %all-reduce.28.cloned.1.call-start = ((), (), s32[]{:S(2)}) async-start(), calls=%async_computation.8 | async-start | bytes 2097152 | tf_op jit(solution)/shard_map/psum | solution.py:276
  85.0 4.8 collective-permute-start
  144.9 8.8 collective-permute-start.1
  154.3 8.3 collective-permute-start.2
  163.3 9.1 collective-permute-start.3
  215.4 145.0 %all-gather.10.cloned.1.call-start = ((), (), s32[]{:S(2)}) async-start(), calls=%async_computation.9 | async-start | bytes 7208960 | tf_op jit(solution)/shard_map/all_gather | solution.py:204
  216.0 179.5 %all-reduce.34.cloned.1.call-start = ((), (), s32[]{:S(2)}) async-start(), calls=%async_computation.18 | async-start | bytes 4194304 | tf_op jit(solution)/shard_map/psum | solution.py:288
  216.5 16.8 %collective-permute-start.4 = (bf16[1408,256]{1,0:T(8,128)(2,1)S(1)}, bf16[1408,256]{1,0:T(8,128)(2,1)}, u32[]{:S(2)}, u32[]{:S(2)}) collective-permute-start(bf16[1408,256]{1,0:T(8,128)(2,1)S(1)} %copy-done.80), channel_id=1, source_target_pairs={{0,8},{8,16},{16,24},{24,0},{1,9},{9,17},{17,25},{25,1},{2,10},{10... | collective-permute-start | bytes 2162696 | tf_op jit(solution)/shard_map/ppermute | solution.py:183
  233.2 19.0 %collective-permute-start.5 = (bf16[1408,256]{1,0:T(8,128)(2,1)}, bf16[1408,256]{1,0:T(8,128)(2,1)}, u32[]{:S(2)}, u32[]{:S(2)}) collective-permute-start(bf16[1408,256]{1,0:T(8,128)(2,1)} %collective-permute-done.4), channel_id=1, source_target_pairs={{0,8},{8,16},{16,24},{24,0},{1,9},{9,17},{17,25},{25,1},{2,10},{10... | collective-permute-start | bytes 2162696 | tf_op jit(solution)/shard_map/ppermute | solution.py:183
  252.2 33.4 %collective-permute-start.6 = (bf16[1408,256]{1,0:T(8,128)(2,1)}, bf16[1408,256]{1,0:T(8,128)(2,1)S(1)}, u32[]{:S(2)}, u32[]{:S(2)}) collective-permute-start(bf16[1408,256]{1,0:T(8,128)(2,1)} %collective-permute-done.5), channel_id=1, source_target_pairs={{0,8},{8,16},{16,24},{24,0},{1,9},{9,17},{17,25},{25,1},{2,10},{10... | collective-permute-start | bytes 2162696 | tf_op jit(solution)/shard_map/ppermute | solution.py:183
  375.7 218.6 %reduce-scatter.13.cloned.1.call-start = ((), (), s32[]{:S(2)}) async-start(), calls=%async_computation.12 | async-start | bytes 2621440 | tf_op jit(solution)/shard_map/reduce_scatter | solution.py:363
  408.6 185.8 %reduce-scatter.17.cloned.1.call-start = ((), (), s32[]{:S(2)}) async-start(), calls=%async_computation.14 | async-start | bytes 7208960 | tf_op jit(solution)/shard_map/reduce_scatter | solution.py:366
  434.6 10.4 collective-permute-start.7
  446.4 10.5 collective-permute-start.8
  458.0 9.9 collective-permute-start.9
  462.8 225.3 %reduce-scatter.11.cloned.1.call-start = ((), (), s32[]{:S(2)}) async-start(), calls=%async_computation.11 | async-start | bytes 7864320 | tf_op jit(solution)/shard_map/reduce_scatter | solution.py:359
  565.3 6.5 collective-permute-start.10
  575.6 310.5 %reduce-scatter.15.cloned.1.call-start = ((), (), s32[]{:S(2)}) async-start(), calls=%async_computation.13 | async-start | bytes 14417920 | tf_op jit(solution)/shard_map/reduce_scatter | solution.py:365
  584.9 326.7 %reduce-scatter.19.cloned.1.call-start = ((), (), s32[]{:S(2)}) async-start(), calls=%async_computation.15 | async-start | bytes 655360
  588.3 343.5 %reduce-scatter.21.cloned.1.call-start = ((), (), s32[]{:S(2)}) async-start(), calls=%async_computation.16 | async-start | bytes 81920
  589.8 362.6 %all-reduce.30.cloned.1.call-start = ((), (), s32[]{:S(2)}) async-start(), calls=%async_computation.10 | async-start | bytes 2097152 | tf_op jit(solution)/shard_map/psum | solution.py:352
  594.3 506.3 %all-reduce.32.cloned.1.call-start = ((), (), s32[]{:S(2)}) async-start(), calls=%async_computation.17 | async-start | bytes 12845056 | tf_op jit(solution)/shard_map/psum | solution.py:369
  (147 other events, 1861.2 us)
Sparse Core Ops, SparseCore 0:
  9.6 72.2 all-gather.5
  83.5 29.3 all-gather.7
  215.5 21.5 all-reduce.27
  238.6 121.7 all-gather.9
  375.8 19.5 all-reduce.33
  408.7 45.0 reduce-scatter.12
  462.9 105.5 reduce-scatter.16
  575.7 112.3 reduce-scatter.10
  690.6 195.4 reduce-scatter.14
  888.9 22.6 reduce-scatter.18
  914.5 17.2 reduce-scatter.20
  934.6 17.7 all-reduce.29
  956.7 143.7 all-reduce.31
